TPU v7x, 512 devices: a whole 4x4x16 slice. The times are simulated.
512 devices in a mesh: aux: 32 (over z, y_hi), pair: 16 (over x, y_lo, core).
Axes of the slice: x: 4, y: 4 (y_hi: 2, y_lo: 2; y = y_hi * 2 + y_lo), z: 16, core: 2. Of those that a mesh axis runs over, the one named last changes fastest.
Arguments:
- half_ints: bfloat16 [96, 1408, 4096], P('pair', None, 'aux'), may hold values from -0.75 to 0.75
- vir_coeffs: bfloat16 [1408, 1280], P(None, 'aux'), may hold values from -0.15625 to 0.15625
- occ_energy: float32 [96], replicated, may hold values from -2 to -0.3
- vir_energy: float32 [1280], replicated, may hold values from 0.3 to 4
- roster: int32 [32, 2], replicated, may hold values from 0 to 15
Outputs:
- density: bfloat16 [1280, 96, 4096], P('pair', 'aux')
All inputs are finite; a program needn't handle non-finite values.
Results may differ from a plain program's by a relative error of at most 0.0058.
Values may be sent and summed in bfloat16 or wider, within the bound.
A program may use at most 64 MiB of HBM per device.

v0:
```python
import jax
import jax.numpy as jnp
from jax import lax
from jax.sharding import PartitionSpec as P

spin_scale = 1.3


def broadcast(value, axis, source):
    kept = jnp.where(lax.axis_index(axis) == source, value, 0).astype(value.dtype)
    return lax.psum(kept, axis)


def per_device(half_ints, vir_coeffs, occ_energy, vir_energy, roster):
    occ_rows = half_ints.shape[0]
    aux_slice = half_ints.shape[2]
    half_flat = jnp.transpose(half_ints, (1, 0, 2)).reshape(
        half_ints.shape[1], occ_rows * aux_slice
    )
    columns = lax.all_gather(vir_coeffs, "aux", axis=1, tiled=True)
    product = jnp.dot(jnp.transpose(columns), half_flat, preferred_element_type=jnp.float32)
    vir_ints = product.astype(jnp.bfloat16).reshape(columns.shape[1], occ_rows, aux_slice)
    by_virtual = lax.all_to_all(vir_ints, "pair", split_axis=0, concat_axis=1, tiled=True)
    aux_count = lax.axis_size("aux")
    aux_index = lax.axis_index("aux")
    pair_index = lax.axis_index("pair")
    vir_width = by_virtual.shape[0]
    occ_width = by_virtual.shape[1] // aux_count
    step_count = roster.shape[1]
    block_plan = lax.dynamic_index_in_dim(roster, aux_index, 0, keepdims=False)
    sources = []
    for position in range(step_count):
        sources.append(lax.dynamic_index_in_dim(block_plan, position, 0, keepdims=False))
    own_block = lax.all_to_all(by_virtual, "aux", split_axis=1, concat_axis=2, tiled=True)
    remotes = [broadcast(own_block, "pair", source) for source in sources]
    aux_total = own_block.shape[2]
    flat_local = own_block.reshape(vir_width * occ_width, aux_total)
    occ_block = lax.dynamic_slice_in_dim(occ_energy, aux_index * occ_width, occ_width, 0)
    vir_block = lax.dynamic_slice_in_dim(vir_energy, pair_index * vir_width, vir_width, 0)
    energy_left = (vir_block[:, None] - occ_block[None, :]).reshape(-1)
    density = jnp.zeros((vir_width * occ_width, aux_total), jnp.float32)
    for position in range(step_count):
        flat_remote = remotes[position].reshape(vir_width * occ_width, aux_total)
        energy_block = lax.dynamic_slice_in_dim(
            vir_energy, sources[position] * vir_width, vir_width, 0
        )
        energy_right = (energy_block[:, None] - occ_block[None, :]).reshape(-1)
        integrals = jnp.dot(
            flat_local, jnp.transpose(flat_remote), preferred_element_type=jnp.float32
        )
        amplitudes = (
            spin_scale * integrals / (energy_left[:, None] + energy_right[None, :])
        ).astype(jnp.bfloat16)
        density = density + jnp.dot(amplitudes, flat_remote, preferred_element_type=jnp.float32)
    return density.astype(jnp.bfloat16).reshape(vir_width, occ_width, aux_total)


def solution(mesh):
    in_specs = (P("pair", None, "aux"), P(None, "aux"), P(), P(), P())
    out_specs = P("pair", "aux", None)
    return jax.shard_map(
        per_device, mesh=mesh, in_specs=in_specs, out_specs=out_specs, check_vma=False
    )
```

profile of v0, /device:TPU:15, one launch (start us, length us, event | category | flops | bytes accessed | tf_op | source)
XLA Modules:
  0.0 497.1 jit_solution(2042534354434699088)
XLA Ops:
  6.5 0.0 copy-start
  6.5 0.0 all-gather.2.cloned.1.call-start
  6.5 0.7 all-gather.2.cloned.1.call-update
  7.3 2.9 copy.14
  10.2 153.8 %all-gather.2.cloned.1.call-done = bf16[1408,1280]{0,1:T(8,128)(2,1)} async-done(((bf16[1408,40]{0,1:T(8,128)(2,1)}), bf16[1408,1280]{0,1:T(8,128)(2,1)}) %all-gather.2.cloned.1.call-update) | async-done | bytes 3604496 | tf_op jit(solution)/shard_map/all_gather | solution.py:20
  164.0 6.4 %convolution_convert_fusion = bf16[1280,768]{0,1:T(8,128)(2,1)} fusion(bf16[1408,1280]{0,1:T(8,128)(2,1)} %all-gather.2.cloned.1.call-done, bf16[1408,768]{0,1:T(8,128)(2,1)S(1)} %bitcast.58), kind=kOutput, calls=%fused_computation.2 | convolution fusion | flops 2769223680 | bytes 7733248 | tf_op jit(solution)/shard_map/dot_general | solution.py:21
  170.4 3.9 copy.15
  174.3 45.4 %all_to_all.33 = bf16[1280,6,128]{2,1,0:T(8,128)(2,1)S(1)} all-to-all(bf16[1280,6,128]{2,1,0:T(8,128)(2,1)S(1)} %copy.15), channel_id=1, replica_groups=mesh['aux'=32,'pair'=16] {'pair'}, dimensions={0} | all-to-all | bytes 3932160 | tf_op jit(solution)/shard_map/all_to_all | solution.py:23
  219.7 1.5 copy.17
  221.2 7.8 %all-to-all-start.1 = ((bf16[80,96,128]{2,0,1:T(8,128)(2,1)}), bf16[80,96,128]{2,0,1:T(8,128)(2,1)S(1)}, u32[]{:S(2)}, u32[]{:S(2)}) async-start(bf16[80,96,128]{2,0,1:T(8,128)(2,1)} %bitcast.55), calls=%async_computation.1 | async-start | bytes 3932160 | tf_op jit(solution)/shard_map/all_to_all | solution.py:34
  229.0 0.2 all-reduce.3.cloned.1.call-start
  229.3 0.0 copy-done
  229.3 0.1 constant_dynamic-slice_fusion
  229.3 0.6 fusion.41
  231.2 89.0 %all-to-all-done.1 = bf16[80,96,128]{2,0,1:T(8,128)(2,1)S(1)} async-done(((bf16[80,96,128]{2,0,1:T(8,128)(2,1)}), bf16[80,96,128]{2,0,1:T(8,128)(2,1)S(1)}, u32[]{:S(2)}, u32[]{:S(2)}) %all-to-all-start.1) | async-done | bytes 1966112 | tf_op jit(solution)/shard_map/all_to_all | solution.py:34
  320.2 0.0 copy-start.1
  320.2 0.3 broadcast_select_fusion
  320.4 1.0 copy-done.1
  321.4 0.5 copy.20
  322.0 0.5 copy.19
  322.5 5.2 %copy_bitcast_fusion = (bf16[240,4096]{1,0:T(8,128)(2,1)}, bf16[240,4096]{1,0:T(8,128)(2,1)}) fusion(bf16[30,8,32,128]{3,2,1,0:T(8,128)(2,1)S(1)} %bitcast.56, bf16[30,8,32,128]{3,2,1,0:T(8,128)(2,1)S(1)} %bitcast.57), kind=kLoop, calls=%fused_computation.3 | loop fusion | bytes 7864320 | tf_op jit(solution)/shard_map/reshape | solution.py:43
  327.7 0.0 copy-start.2
  327.7 0.0 all-reduce.3.cloned.1.call-update
  329.0 0.0 copy-done.2
  329.0 0.1 dynamic_slice.26
  329.1 0.9 fusion.40
  329.9 0.1 broadcast_subtract_fusion
  330.1 0.2 sub.65
  330.2 0.2 sub.59
  330.4 0.2 sub.62
  330.5 2.1 copy.18
  332.6 137.9 %all-reduce.3.cloned.1.call-done = (bf16[240,4096]{1,0:T(8,128)(2,1)}, bf16[240,4096]{1,0:T(8,128)(2,1)}) async-done(((bf16[240,4096]{1,0:T(8,128)(2,1)}, bf16[240,4096]{1,0:T(8,128)(2,1)}), (bf16[240,4096]{1,0:T(8,128)(2,1)}, bf16[240,4096]{1,0:T(8,128)(2,1)})) %all-reduce.3.cloned.1.call-update) | async-done | bytes 3932176 | tf_op jit(solution)/shard_map/psum | solution.py:11
  470.5 6.4 %fusion.26 = f32[240,4096]{1,0:T(8,128)} fusion(bf16[240,4096]{1,0:T(8,128)(2,1)} %get-tuple-element.5, bf16[30,8,32,128]{3,2,1,0:T(8,128)(2,1)S(1)} %bitcast.50, f32[240]{0:T(256)S(1)} %sub.62, f32[240]{0:T(256)S(1)} %sub.59), kind=kOutput, calls=%fused_computation.19 | convolution fusion | flops 943948800 | bytes 7866240 | tf_op jit(solution)/shard_map/dot_general | solution.py:54
  476.8 7.0 %fusion = bf16[240,4096]{1,0:T(8,128)(2,1)} fusion(f32[240,4096]{1,0:T(8,128)} %fusion.26, bf16[240,4096]{1,0:T(8,128)(2,1)} %get-tuple-element.6, bf16[30,8,32,128]{3,2,1,0:T(8,128)(2,1)S(1)} %bitcast.51, f32[240]{0:T(256)S(1)} %sub.65, f32[240]{0:T(256)S(1)} %sub.59), kind=kOutput, calls=%fused_computation.1 | convolution fusion | flops 945914880 | bytes 9832320 | tf_op jit(solution)/shard_map/dot_general | solution.py:54
  483.8 3.7 reshape.80
  487.5 2.7 copy.21
Async XLA Ops:
  6.5 222.7 %copy-start = (s32[32,2]{0,1:T(2,128)S(1)}, s32[32,2]{0,1:T(2,128)}, u32[]{:S(2)}) copy-start(s32[32,2]{0,1:T(2,128)} %param.9) | copy-start | bytes 772
  6.5 157.5 %all-gather.2.cloned.1.call-start = ((), (), s32[]{:S(2)}) async-start(), calls=%async_computation.2 | async-start | bytes 3717120 | tf_op jit(solution)/shard_map/all_gather | solution.py:20
  221.2 99.0 %all-to-all-start.1 = ((bf16[80,96,128]{2,0,1:T(8,128)(2,1)}), bf16[80,96,128]{2,0,1:T(8,128)(2,1)S(1)}, u32[]{:S(2)}, u32[]{:S(2)}) async-start(bf16[80,96,128]{2,0,1:T(8,128)(2,1)} %bitcast.55), calls=%async_computation.1 | async-start | bytes 3932160 | tf_op jit(solution)/shard_map/all_to_all | solution.py:34
  229.0 241.4 %all-reduce.3.cloned.1.call-start = ((), (), s32[]{:S(2)}) async-start(), calls=%async_computation.3 | async-start | bytes 7864320 | tf_op jit(solution)/shard_map/psum | solution.py:11
  320.2 1.3 copy-start.1
  327.7 1.3 copy-start.2
Sparse Core Ops, SparseCore 0:
  10.5 153.4 all-gather.1
  327.9 142.5 all-reduce.2
where the time goes:
time: 498 us; the launch traced here: 497 us
  waiting for transfers between devices  381 us (77%)
  blocking collectives  45.4 us (9%)
  local copies, waits for them, and re-layouts  26.1 us (5%)
  matrix products  19.8 us (4%)
  between operations  16 us (3%)
  starting transfers between devices  8.03 us (2%)
    all_gather x1, waiting for transfers between devices, per_device(): columns = lax.all_gather(vir_coeffs, 'aux', axis=1, tiled=True)  154 us
    psum x1, waiting for transfers between devices, broadcast(): return lax.psum(kept, axis)  138 us
    all_to_all x1, waiting for transfers between devices, per_device(): lax.all_to_all(by_virtual, 'aux', split_axis=1, concat_axis=2, tiled=True)  89 us
    all_to_all x1, blocking collectives, per_device(): lax.all_to_all(vir_ints, 'pair', split_axis=0, concat_axis=1, tiled=True)  45.4 us
    dot_general x2, matrix products, per_device(): jnp.dot(amplitudes, flat_remote, preferred_element_type=jnp.float32)  13.3 us
  transfers between devices with their start and end apart: 3, of which 3 were waited for; matrix products, arithmetic and copies ran while one was open for 1% of the time, Pallas kernels for 0%

commit v1 on v0

v1 whole, which is shorter than its diff:
```python
import jax
import jax.numpy as jnp
from jax import lax
from jax.experimental import pallas as pl
from jax.experimental.pallas import tpu as pltpu
from jax.sharding import PartitionSpec as P

spin_scale = 1.3
MESH = pl.DeviceIdType.MESH
ANY = pl.BlockSpec(memory_space=pl.ANY)
DMA = pltpu.SemaphoreType.DMA

GROUP = 384


def place():
    aux, pair = lax.axis_index("aux"), lax.axis_index("pair")
    return aux // 2, aux % 2, pair // 4, (pair // 2) % 2, pair % 2, aux, pair


def chip_of(c):
    return c // 8, (c // 4) % 2, c % 4


def remote(src, dst, send, recv, device):
    return pltpu.make_async_remote_copy(
        src_ref=src, dst_ref=dst, send_sem=send, recv_sem=recv,
        device_id=device, device_id_type=MESH,
    )


def signal(device):
    pl.semaphore_signal(
        pltpu.get_barrier_semaphore(), inc=1, device_id=device, device_id_type=MESH
    )


def gather_kernel(src, out, own_sem, send_z, recv_z, send_p, recv_p, send_c, recv_c):
    z, h, x, yl, core, aux, pair = place()
    w = yl * 2 + core
    chip = (h * 2 + yl) * 4 + x
    partner = (aux, pair + 1 - 2 * core)

    def z_peer(d):
        return (((z + d) % 16) * 2 + h, pair)

    def chip_peer(e):
        ph, pyl, px = chip_of((chip + e) % 16)
        return (z * 2 + ph, px * 4 + pyl * 2 + core)

    def region(c, at_core):
        ch, cyl, cx = chip_of(c)
        columns = pl.ds(pl.multiple_of(cx * GROUP, 128), GROUP)
        return out.at[:, (cyl * 2 + at_core) * 2 + ch, :, columns]

    @pl.loop(1, 16)
    def _(d):
        signal(z_peer(d))
        signal(chip_peer(d))

    signal(partner)
    pl.semaphore_wait(pltpu.get_barrier_semaphore(), 31)

    mine = pl.ds(pl.multiple_of(x * GROUP, 128), GROUP)

    def slot(t):
        return out.at[t, w * 2 + h, :, mine]

    owner = z % 4 == w

    @pl.when(owner)
    def _():
        @pl.loop(1, 16)
        def _(d):
            remote(src.at[:, mine], slot(z // 4), send_z.at[d], recv_z.at[z // 4], z_peer(d)).start()

        copy = pltpu.make_async_copy(src.at[:, mine], slot(z // 4), own_sem)
        copy.start()
        copy.wait()

    @pl.loop(0, 4)
    def _(t):
        @pl.when(jnp.logical_or(jnp.logical_not(owner), t != z // 4))
        def _():
            remote(slot(t), slot(t), send_z.at[0], recv_z.at[t], partner).wait_recv()

    @pl.loop(1, 16)
    def _(e):
        remote(region(chip, core), region(chip, core), send_p.at[e], recv_p.at[chip], chip_peer(e)).start()

    remote(region(chip, core), region(chip, core), send_c.at[chip], recv_c.at[chip], partner).start()

    @pl.loop(1, 16)
    def _(e):
        c = (chip + 16 - e) % 16
        part = region(c, core)
        remote(part, part, send_c.at[c], recv_p.at[c], partner).wait_recv()
        remote(part, part, send_c.at[c], recv_c.at[c], partner).start()

    @pl.loop(0, 16)
    def _(c):
        part = region(c, 1 - core)
        remote(part, part, send_c.at[c], recv_c.at[c], partner).wait()

    @pl.loop(1, 16)
    def _(e):
        part = region(chip, core)
        remote(part, part, send_p.at[e], recv_p.at[chip], chip_peer(e)).wait_send()

    @pl.when(owner)
    def _():
        @pl.loop(1, 16)
        def _(d):
            remote(src.at[:, mine], slot(z // 4), send_z.at[d], recv_z.at[0], z_peer(d)).wait_send()


def gather_columns(rows):
    return pl.pallas_call(
        gather_kernel,
        out_shape=jax.ShapeDtypeStruct((4, 8) + rows.shape, rows.dtype),
        in_specs=[ANY],
        out_specs=ANY,
        scratch_shapes=[DMA, DMA((16,)), DMA((4,)), DMA((16,)), DMA((16,)), DMA((16,)), DMA((16,))],
        compiler_params=pltpu.CompilerParams(collective_id=0, has_side_effects=True),
        name="gather_columns",
    )(rows)


def transform_kernel(coeff, half, out):
    wide = jnp.concatenate([half[i] for i in range(6)], axis=1)
    product = jnp.dot(coeff[...], wide, preferred_element_type=jnp.float32)
    product = product.astype(jnp.bfloat16)
    for v in range(out.shape[0]):
        for i in range(6):
            out[v, i // 3, i % 3] = product[80 * v : 80 * v + 80, 128 * i : 128 * i + 128]


def transform(coeff, half):
    steps = 4
    rows = 1280 // steps
    return pl.pallas_call(
        transform_kernel,
        out_shape=jax.ShapeDtypeStruct((16, 2, 3, 80, 128), jnp.bfloat16),
        grid=(steps,),
        in_specs=[
            pl.BlockSpec((rows, 1408), lambda g: (g, 0)),
            pl.BlockSpec((6, 1408, 128), lambda g: (0, 0, 0)),
        ],
        out_specs=pl.BlockSpec((16 // steps, 2, 3, 80, 128), lambda g: (g, 0, 0, 0, 0)),
        name="transform",
    )(coeff, half)


def select_kernel(plan, block, out):
    out[0] = block[0, 0]


def select(plan, vir):
    return pl.pallas_call(
        select_kernel,
        out_shape=jax.ShapeDtypeStruct((2, 6, 80, 128), jnp.bfloat16),
        grid_spec=pltpu.PrefetchScalarGridSpec(
            num_scalar_prefetch=1,
            grid=(2, 2),
            in_specs=[pl.BlockSpec((1, 1, 3, 80, 128), lambda h, s, plan: (plan[h, s], h, 0, 0, 0))],
            out_specs=pl.BlockSpec((1, 3, 80, 128), lambda h, s, plan: (h, s, 0, 0)),
        ),
        name="select",
    )(plan, vir)


def exchange_kernel(
    vir, chosen, local, paired, relay, relay_r, own_sem, send_v, recv_v, send_w, recv_w,
    send_x, recv_x, send_r, recv_r, send_g, recv_g, send_c, recv_c,
):
    z, h, x, yl, core, aux, pair = place()
    partner = (aux, pair + 1 - 2 * core)
    own = pl.ds(pl.multiple_of(aux * 128, 128), 128)
    q_own = pair // 2

    @pl.loop(1, 16)
    def _(d):
        signal((aux, (pair + d) % 16))

    @pl.loop(1, 32)
    def _(d):
        signal(((aux + d) % 32, pair))

    pl.semaphore_wait(pltpu.get_barrier_semaphore(), 46)

    def chip_pair(q):
        return q * 2 + core

    def spread(q, at_core):
        first = (q * 2 + at_core + 16 - z) % 16
        return paired.at[:, :, pl.ds(pl.multiple_of(first * 256, 128), 256)]

    def chosen_out():
        return remote(chosen, relay_r, send_w, recv_w, (aux, (pair + z) % 16))

    @pl.when(z != 0)
    def _():
        chosen_out().start()

    def vir_out(n):
        v = (pair + n) % 16
        return remote(vir.at[v], relay.at[pair], send_v.at[n], recv_v.at[pair], (aux, v))

    @pl.loop(0, 16)
    def _(n):
        turn = (n + z) % 16

        @pl.when(turn != 0)
        def _():
            vir_out(turn).start()

    def onward(src, dst, send, recv, plane, to_h, home_sem):
        at_home = jnp.logical_and(plane == z, to_h == h)

        @pl.when(at_home)
        def _():
            pltpu.make_async_copy(src, dst, home_sem).start()

        @pl.when(jnp.logical_not(at_home))
        def _():
            remote(src, dst, send, recv, (plane * 2 + to_h, pair)).start()

    plane_r = (pair + 16 - z) % 16

    def chosen_on(src):
        @pl.loop(0, 2)
        def _(to_h):
            onward(src.at[to_h], paired.at[:, :, own], send_r.at[to_h], recv_r.at[h], plane_r, to_h, own_sem.at[0])

    @pl.when(z == 0)
    def _():
        chosen_on(chosen)

    @pl.when(z != 0)
    def _():
        chosen_out().wait_recv()
        chosen_on(relay_r)

    @pl.loop(0, 16)
    def _(n):
        turn = (n + z) % 16
        plane = (pair + 16 - turn) % 16

        def forward(src):
            @pl.loop(0, 2)
            def _(to_h):
                onward(
                    src.at[to_h], local.at[:, :, own], send_x.at[plane * 2 + to_h],
                    recv_x.at[aux], plane, to_h, own_sem.at[1],
                )

        @pl.when(turn == 0)
        def _():
            forward(vir.at[pair])

        @pl.when(turn != 0)
        def _():
            remote(relay.at[plane], relay.at[plane], send_v.at[0], recv_v.at[plane], partner).wait_recv()
            forward(relay.at[plane])

    @pl.loop(0, 2)
    def _(from_h):
        home = jnp.logical_and(plane_r == z, from_h == h)
        first = (pair + 16 - z) % 16
        part = paired.at[:, :, pl.ds(pl.multiple_of((first * 2 + from_h) * 128, 128), 128)]

        @pl.when(home)
        def _():
            pltpu.make_async_copy(chosen.at[0], part, own_sem.at[0]).wait()

        @pl.when(jnp.logical_not(home))
        def _():
            remote(part, part, send_r.at[0], recv_r.at[from_h], partner).wait_recv()

    mine = spread(q_own, core)

    @pl.loop(1, 8)
    def _(e):
        remote(mine, mine, send_g.at[e], recv_g.at[q_own], (aux, chip_pair((q_own + e) % 8))).start()

    remote(mine, mine, send_c.at[q_own], recv_c.at[q_own], partner).start()

    @pl.loop(1, 8)
    def _(e):
        q = (q_own + 8 - e) % 8
        part = spread(q, core)
        remote(part, part, send_c.at[q], recv_g.at[q], partner).wait_recv()
        remote(part, part, send_c.at[q], recv_c.at[q], partner).start()

    @pl.loop(0, 8)
    def _(q):
        part = spread(q, 1 - core)
        remote(part, part, send_c.at[q], recv_c.at[q], partner).wait()

    @pl.loop(1, 8)
    def _(e):
        remote(mine, mine, send_g.at[e], recv_g.at[q_own], (aux, chip_pair((q_own + e) % 8))).wait_send()

    @pl.when(z != 0)
    def _():
        chosen_out().wait_send()

    @pl.loop(1, 16)
    def _(n):
        vir_out(n).wait_send()

    @pl.loop(0, 2)
    def _(to_h):
        @pl.when(jnp.logical_not(jnp.logical_and(plane_r == z, to_h == h)))
        def _():
            part = paired.at[:, :, own]
            remote(chosen.at[to_h], part, send_r.at[to_h], recv_r.at[0], partner).wait_send()

    @pl.loop(0, 32)
    def _(a):
        part = local.at[:, :, pl.ds(pl.multiple_of(a * 128, 128), 128)]

        @pl.when(a == aux)
        def _():
            pltpu.make_async_copy(vir.at[0, 0], part, own_sem.at[1]).wait()

        @pl.when(a != aux)
        def _():
            remote(vir.at[0, 0], part, send_x.at[a], recv_x.at[a], partner).wait()


def exchange(vir, chosen):
    return pl.pallas_call(
        exchange_kernel,
        out_shape=(
            jax.ShapeDtypeStruct((3, 80, 4096), jnp.bfloat16),
            jax.ShapeDtypeStruct((6, 80, 4096), jnp.bfloat16),
        ),
        in_specs=[ANY, ANY],
        out_specs=(ANY, ANY),
        scratch_shapes=[
            pltpu.VMEM((16, 2, 3, 80, 128), jnp.bfloat16),
            pltpu.VMEM((2, 6, 80, 128), jnp.bfloat16),
            DMA((2,)), DMA((16,)), DMA((16,)), DMA, DMA,
            DMA((32,)), DMA((32,)), DMA((2,)), DMA((2,)),
            DMA((8,)), DMA((8,)), DMA((8,)), DMA((8,)),
        ],
        compiler_params=pltpu.CompilerParams(collective_id=1, has_side_effects=True),
        name="exchange",
    )(vir, chosen)


def per_device(half_ints, vir_coeffs, occ_energy, vir_energy, roster):
    aux, pair = lax.axis_index("aux"), lax.axis_index("pair")
    rows = jnp.pad(jnp.transpose(vir_coeffs), ((0, 0), (0, 4 * GROUP - vir_coeffs.shape[0])))
    columns = gather_columns(rows).reshape(1280, 4 * GROUP)
    vir = transform(columns, half_ints)
    plan = lax.dynamic_slice_in_dim(roster, pair * 2, 2, 0)
    local, paired = exchange(vir, select(plan, vir))
    flat_local = local.reshape(240, 4096)
    paired = paired.reshape(2, 240, 4096)
    occ_block = lax.dynamic_slice_in_dim(occ_energy, aux * 3, 3, 0)
    vir_block = lax.dynamic_slice_in_dim(vir_energy, pair * 80, 80, 0)
    energy_left = (vir_block[None, :] - occ_block[:, None]).reshape(-1)
    block_plan = lax.dynamic_index_in_dim(roster, aux, 0, keepdims=False)
    density = jnp.zeros((240, 4096), jnp.float32)
    for step in range(2):
        energy_block = lax.dynamic_slice_in_dim(vir_energy, block_plan[step] * 80, 80, 0)
        energy_right = (energy_block[None, :] - occ_block[:, None]).reshape(-1)
        integrals = lax.dot_general(
            flat_local, paired[step], (((1,), (1,)), ((), ())), preferred_element_type=jnp.float32
        )
        amplitudes = (
            spin_scale * integrals / (energy_left[:, None] + energy_right[None, :])
        ).astype(jnp.bfloat16)
        density = density + jnp.dot(amplitudes, paired[step], preferred_element_type=jnp.float32)
    return jnp.transpose(density.astype(jnp.bfloat16).reshape(3, 80, 4096), (1, 0, 2))


def solution(mesh):
    in_specs = (P("pair", None, "aux"), P(None, "aux"), P(), P(), P())
    out_specs = P("pair", "aux", None)
    return jax.shard_map(
        per_device, mesh=mesh, in_specs=in_specs, out_specs=out_specs, check_vma=False
    )
```

time: 498 us -> 225 us (0.45)
  the two profiles are of different devices: /device:TPU:15 before, /device:TPU:7 now
where the time goes in v1:
time: 225 us
  Pallas kernels  202 us (90%)
  matrix products  13.2 us (6%)
  local copies, waits for them, and re-layouts  8.55 us (4%)
    pallas_call x1, Pallas kernels, exchange(): pl.pallas_call(exchange_kernel, out_shape=(jax.ShapeDtypeStruct((3, 80, 4...  140 us
    pallas_call x1, Pallas kernels, gather_columns(): pl.pallas_call(gather_kernel, out_shape=jax.ShapeDtypeStruct((4, 8) + row...  51.5 us
    dot_general x2, matrix products, per_device(): jnp.dot(amplitudes, paired[step], preferred_element_type=jnp.float32)  13.2 us
    pallas_call x1, Pallas kernels, transform(): pl.pallas_call(transform_kernel, out_shape=jax.ShapeDtypeStruct((16, 2, 3...  6.93 us

profile of v1, /device:TPU:7, one launch (start us, length us, event | category | flops | bytes accessed | tf_op | source)
XLA Modules:
  0.0 224.7 jit_solution(16725241591437389398)
XLA Ops:
  0.0 0.0 copy-start
  0.0 0.7 dynamic_slice.21
  0.7 0.0 copy-done
  0.7 0.1 constant_dynamic-slice_fusion
  0.8 0.5 fusion.18
  2.6 0.9 fusion.17
  3.5 0.1 constant_dynamic-slice_fusion.1
  3.5 0.7 copy.7.plan
  4.2 0.1 broadcast_subtract_fusion
  4.3 0.1 sub.65
  4.4 0.1 sub.59
  4.4 0.1 sub.62
  4.5 1.6 pad.4.src
  6.1 51.5 %gather_columns.1 = bf16[4,8,40,1536]{3,2,1,0:T(8,128)(2,1)} custom-call(bf16[40,1536]{1,0:T(8,128)(2,1)} %pad.4.src), custom_call_target="tpu_custom_call" | custom-call | tf_op jit(solution)/shard_map/gather_columns/pallas_call | solution.py:118
  57.6 6.9 %transform.1.block.vir = bf16[16,2,3,80,128]{4,3,2,1,0:T(8,128)(2,1)} custom-call(bf16[1280,1536]{1,0:T(8,128)(2,1)} %bitcast.18, bf16[6,1408,128]{2,1,0:T(8,128)(2,1)} %half.1), custom_call_target="tpu_custom_call" | custom-call | tf_op jit(solution)/shard_map/transform/pallas_call | solution.py:141
  64.5 3.6 %select.2.chosen = bf16[2,6,80,128]{3,2,1,0:T(8,128)(2,1)} custom-call(s32[2,2]{1,0:T(2,128)} %copy.7.plan, bf16[16,2,3,80,128]{4,3,2,1,0:T(8,128)(2,1)} %transform.1.block.vir), custom_call_target="tpu_custom_call" | custom-call | tf_op jit(solution)/shard_map/select/pallas_call | solution.py:159
  68.1 139.7 %exchange.1 = (bf16[3,80,4096]{2,1,0:T(8,128)(2,1)}, bf16[6,80,4096]{2,1,0:T(8,128)(2,1)}) custom-call(bf16[16,2,3,80,128]{4,3,2,1,0:T(8,128)(2,1)} %transform.1.block.vir, bf16[2,6,80,128]{3,2,1,0:T(8,128)(2,1)} %select.2.chosen), custom_call_target="tpu_custom_call" | custom-call | tf_op jit(solution)/shard_map/exchange/pallas_call | solution.py:333
  207.8 3.8 %fusion.16 = (bf16[3,80,4096]{2,1,0:T(8,128)(2,1)S(1)}, bf16[3,80,4096]{2,1,0:T(8,128)(2,1)}) fusion(bf16[6,80,4096]{2,1,0:T(8,128)(2,1)} %get-tuple-element.8), kind=kLoop, calls=%fused_computation.24 | loop fusion | bytes 7864320 | tf_op jit(solution)/shard_map/slice | solution.py:371
  211.5 6.9 %fusion.5 = f32[240,4096]{1,0:T(8,128)} fusion(bf16[240,4096]{1,0:T(8,128)(2,1)} %bitcast.17, bf16[240,4096]{1,0:T(8,128)(2,1)} %bitcast.19, f32[240]{0:T(256)S(1)} %sub.62, f32[240]{0:T(256)S(1)} %sub.59), kind=kOutput, calls=%fused_computation.8 | convolution fusion | flops 943948800 | bytes 7866240 | tf_op jit(solution)/shard_map/dot_general | solution.py:376
  218.4 6.3 %fusion = bf16[240,4096]{1,0:T(8,128)(2,1)} fusion(f32[240,4096]{1,0:T(8,128)} %fusion.5, bf16[240,4096]{1,0:T(8,128)(2,1)S(1)} %bitcast.16, bf16[240,4096]{1,0:T(8,128)(2,1)} %bitcast.20, f32[240]{0:T(256)S(1)} %sub.65, f32[240]{0:T(256)S(1)} %sub.59), kind=kOutput, calls=%fused_computation.1 | convolution fusion | flops 945914880 | bytes 9832320 | tf_op jit(solution)/shard_map/dot_general | solution.py:376
Async XLA Ops:
  0.0 0.7 copy-start

commit v2 on v0

v2 whole, which is shorter than its diff:
```python
import jax
import jax.numpy as jnp
from jax import lax
from jax.experimental import pallas as pl
from jax.experimental.pallas import tpu as pltpu
from jax.sharding import PartitionSpec as P

spin_scale = 1.3
MESH = pl.DeviceIdType.MESH
ANY = pl.BlockSpec(memory_space=pl.ANY)
DMA = pltpu.SemaphoreType.DMA

GROUP = 384


def place():
    aux, pair = lax.axis_index("aux"), lax.axis_index("pair")
    return aux // 2, aux % 2, pair // 4, (pair // 2) % 2, pair % 2, aux, pair


def remote(src, dst, send, recv, device):
    return pltpu.make_async_remote_copy(
        src_ref=src, dst_ref=dst, send_sem=send, recv_sem=recv,
        device_id=device, device_id_type=MESH,
    )


def signal(device):
    pl.semaphore_signal(
        pltpu.get_barrier_semaphore(), inc=1, device_id=device, device_id_type=MESH
    )


def front_kernel(
    plan, rows, half_hbm, local, paired, columns, half, coeff, vir, relay, chosen, relay_r,
    half_sem, own_sem, home_sem, send_z, recv_z, send_p, recv_p, send_k, recv_k,
    send_v, recv_v, send_w, recv_w, send_x, recv_x, send_r, recv_r, send_g, recv_g, send_c, recv_c,
):
    z, h, x, yl, core, aux, pair = place()
    w = yl * 2 + core
    side = h * 4 + x
    partner = (aux, pair + 1 - 2 * core)
    own = pl.ds(pl.multiple_of(aux * 128, 128), 128)
    q_own = pair // 2

    half_load = pltpu.make_async_copy(half_hbm, half, half_sem)
    half_load.start()

    @pl.loop(1, 16)
    def _(d):
        signal((aux, (pair + d) % 16))

    @pl.loop(1, 32)
    def _(d):
        signal(((aux + d) % 32, pair))

    @pl.loop(1, 8)
    def _(d):
        signal((z * 2 + 1 - h, ((q_own + d) % 8) * 2 + core))

    pl.semaphore_wait(pltpu.get_barrier_semaphore(), 53)

    def z_peer(d):
        return (((z + d) % 16) * 2 + h, pair)

    def piece(ch, cyl, cx, at_core, t):
        first = pl.multiple_of((8 * t + 2 * (cyl * 2 + at_core) + ch) * 40, 8)
        return columns.at[pl.ds(first, 40), pl.ds(pl.multiple_of(cx * GROUP, 128), GROUP)]

    def mine(t):
        return piece(h, yl, x, core, t)

    row_part = rows.at[:, pl.ds(pl.multiple_of(x * GROUP, 128), GROUP)]
    owner = z % 4 == w

    @pl.when(owner)
    def _():
        @pl.loop(1, 16)
        def _(d):
            remote(row_part, mine(z // 4), send_z.at[d], recv_z.at[z // 4], z_peer(d)).start()

        copy = pltpu.make_async_copy(row_part, mine(z // 4), home_sem.at[0])
        copy.start()
        copy.wait()

    def to_chip(e, t):
        other = (side + e) % 8
        device = (z * 2 + other // 4, (other % 4) * 4 + ((yl + e // 8) % 2) * 2 + core)
        return remote(mine(t), mine(t), send_p.at[e, t], recv_p.at[yl * 8 + side, t], device)

    def to_partner(cyl, cside, t):
        part = piece(cside // 4, cyl, cside % 4, core, t)
        return remote(part, part, send_k.at[cyl * 8 + cside, t], recv_k.at[cyl * 8 + cside, t], partner)

    @pl.loop(0, 4)
    def _(t):
        @pl.when(jnp.logical_or(jnp.logical_not(owner), t != z // 4))
        def _():
            remote(mine(t), mine(t), send_z.at[0], recv_z.at[t], partner).wait_recv()

        @pl.loop(1, 8)
        def _(e):
            to_chip(e, t).start()

        to_partner(yl, side, t).start()

    @pl.loop(0, 4)
    def _(t):
        @pl.loop(8, 16)
        def _(e):
            to_chip(e, t).start()

    half_load.wait()

    def vir_out(v):
        return remote(vir.at[v], relay.at[pair], send_v.at[v], recv_v.at[pair], (aux, v))

    def turn_of(g):
        return (w + (1 - 2 * core) * (g // 2) + 2 * (g % 2)) % 4

    def onward(src, dst, send, recv, plane, to_h, sem):
        at_home = jnp.logical_and(plane == z, to_h == h)

        @pl.when(at_home)
        def _():
            pltpu.make_async_copy(src, dst, sem).start()

        @pl.when(jnp.logical_not(at_home))
        def _():
            remote(src, dst, send, recv, (plane * 2 + to_h, pair)).start()

    def forward(g):
        @pl.loop(0, 4)
        def _(n):
            plane = ((x + n + z) % 4) * 4 + turn_of(g)

            def both(src):
                @pl.loop(0, 2)
                def _(to_h):
                    onward(
                        src.at[to_h], local.at[:, :, own], send_x.at[plane * 2 + to_h],
                        recv_x.at[aux], plane, to_h, home_sem.at[1],
                    )

            @pl.when(plane == pair)
            def _():
                both(vir.at[pair])

            @pl.when(plane != pair)
            def _():
                remote(relay.at[plane], relay.at[plane], send_v.at[0], recv_v.at[plane], partner).wait_recv()
                both(relay.at[plane])

    @pl.loop(0, 4)
    def _(g):
        w_now = turn_of(g)
        yl_now = (yl + g % 2) % 2

        @pl.loop(0, 8)
        def _(other):
            @pl.loop(0, 4)
            def _(t):
                @pl.when(jnp.logical_and(g < 2, jnp.logical_or(g == 1, other != side)))
                def _():
                    part = piece(other // 4, yl_now, other % 4, core, t)
                    remote(part, part, send_p.at[0, 0], recv_p.at[yl_now * 8 + other, t], partner).wait_recv()
                    to_partner(yl_now, other, t).start()

                @pl.when(g >= 2)
                def _():
                    part = piece(other // 4, yl_now, other % 4, 1 - core, t)
                    remote(part, part, send_p.at[0, 0], recv_k.at[yl_now * 8 + other, t], partner).wait_recv()

        def load(t):
            first = pl.multiple_of((4 * t + w_now) * 80, 16)
            return pltpu.make_async_copy(columns.at[pl.ds(first, 80), pl.ds(0, 1408)], coeff.at[t], own_sem.at[t])

        for t in range(4):
            load(t).start()
        for t in range(4):
            load(t).wait()
        wide = jnp.concatenate([half[i] for i in range(6)], axis=1)
        product = jnp.dot(coeff[...].reshape(320, 1408), wide, preferred_element_type=jnp.float32)
        product = product.astype(jnp.bfloat16)
        for t in range(4):
            for i in range(6):
                vir[4 * t + w_now, i // 3, i % 3] = product[80 * t : 80 * t + 80, 128 * i : 128 * i + 128]

        @pl.loop(0, 4)
        def _(n):
            v = ((x + n + 4 - z % 4) % 4) * 4 + w_now

            @pl.when(v != pair)
            def _():
                vir_out(v).start()

        @pl.when(g == 0)
        def _():
            forward(0)

    for to_h in range(2):
        for step in range(2):
            chosen[to_h, 3 * step : 3 * step + 3] = vir[plan[to_h, step], to_h]

    def chosen_out():
        return remote(chosen, relay_r, send_w, recv_w, (aux, (pair + z) % 16))

    plane_r = (pair + 16 - z) % 16

    def chosen_on(src):
        @pl.loop(0, 2)
        def _(to_h):
            onward(src.at[to_h], paired.at[:, :, own], send_r.at[to_h], recv_r.at[h], plane_r, to_h, home_sem.at[0])

    @pl.when(z == 0)
    def _():
        chosen_on(chosen)

    @pl.when(z != 0)
    def _():
        chosen_out().start()
        chosen_out().wait_recv()
        chosen_on(relay_r)

    @pl.loop(1, 4)
    def _(g):
        forward(g)

    def spread(q, at_core):
        first = (q * 2 + at_core + 16 - z) % 16
        return paired.at[:, :, pl.ds(pl.multiple_of(first * 256, 128), 256)]

    def spread_out(e):
        part = spread(q_own, core)
        return remote(part, part, send_g.at[e], recv_g.at[q_own], (aux, ((q_own + e) % 8) * 2 + core))

    @pl.loop(0, 2)
    def _(from_h):
        home = jnp.logical_and(plane_r == z, from_h == h)
        part = paired.at[:, :, pl.ds(pl.multiple_of((plane_r * 2 + from_h) * 128, 128), 128)]

        @pl.when(home)
        def _():
            pltpu.make_async_copy(chosen.at[0], part, home_sem.at[0]).wait()

        @pl.when(jnp.logical_not(home))
        def _():
            remote(part, part, send_r.at[0], recv_r.at[from_h], partner).wait_recv()

    @pl.loop(1, 8)
    def _(e):
        spread_out(e).start()

    part = spread(q_own, core)
    remote(part, part, send_c.at[q_own], recv_c.at[q_own], partner).start()

    @pl.loop(1, 8)
    def _(e):
        q = (q_own + 8 - e) % 8
        part = spread(q, core)
        remote(part, part, send_c.at[q], recv_g.at[q], partner).wait_recv()
        remote(part, part, send_c.at[q], recv_c.at[q], partner).start()

    @pl.loop(0, 8)
    def _(q):
        part = spread(q, 1 - core)
        remote(part, part, send_c.at[q], recv_c.at[q], partner).wait()

    @pl.loop(1, 8)
    def _(e):
        spread_out(e).wait_send()

    @pl.when(owner)
    def _():
        @pl.loop(1, 16)
        def _(d):
            remote(row_part, mine(z // 4), send_z.at[d], recv_z.at[0], z_peer(d)).wait_send()

    @pl.loop(0, 4)
    def _(t):
        @pl.loop(1, 16)
        def _(e):
            to_chip(e, t).wait_send()

        @pl.loop(0, 16)
        def _(c):
            to_partner(c // 8, c % 8, t).wait_send()

    @pl.when(z != 0)
    def _():
        chosen_out().wait_send()

    @pl.loop(0, 16)
    def _(v):
        @pl.when(v != pair)
        def _():
            vir_out(v).wait_send()

    @pl.loop(0, 2)
    def _(to_h):
        @pl.when(jnp.logical_not(jnp.logical_and(plane_r == z, to_h == h)))
        def _():
            part = paired.at[:, :, own]
            remote(chosen.at[to_h], part, send_r.at[to_h], recv_r.at[0], partner).wait_send()

    @pl.loop(0, 32)
    def _(a):
        part = local.at[:, :, pl.ds(pl.multiple_of(a * 128, 128), 128)]

        @pl.when(a == aux)
        def _():
            pltpu.make_async_copy(vir.at[0, 0], part, home_sem.at[1]).wait()

        @pl.when(a != aux)
        def _():
            remote(vir.at[0, 0], part, send_x.at[a], recv_x.at[a], partner).wait()


def front(plan, rows, half):
    bf16 = jnp.bfloat16
    return pl.pallas_call(
        front_kernel,
        out_shape=(
            jax.ShapeDtypeStruct((3, 80, 4096), bf16),
            jax.ShapeDtypeStruct((6, 80, 4096), bf16),
            jax.ShapeDtypeStruct((1280, 4 * GROUP), bf16),
        ),
        in_specs=[pl.BlockSpec(memory_space=pltpu.SMEM), ANY, ANY],
        out_specs=(ANY, ANY, ANY),
        scratch_shapes=[
            pltpu.VMEM((6, 1408, 128), bf16),
            pltpu.VMEM((4, 80, 1408), bf16),
            pltpu.VMEM((16, 2, 3, 80, 128), bf16),
            pltpu.VMEM((16, 2, 3, 80, 128), bf16),
            pltpu.VMEM((2, 6, 80, 128), bf16),
            pltpu.VMEM((2, 6, 80, 128), bf16),
            DMA, DMA((4,)), DMA((2,)),
            DMA((16,)), DMA((4,)), DMA((16, 4)), DMA((16, 4)), DMA((16, 4)), DMA((16, 4)),
            DMA((16,)), DMA((16,)), DMA, DMA,
            DMA((32,)), DMA((32,)), DMA((2,)), DMA((2,)),
            DMA((8,)), DMA((8,)), DMA((8,)), DMA((8,)),
        ],
        compiler_params=pltpu.CompilerParams(collective_id=0, has_side_effects=True),
        name="front",
    )(plan, rows, half)


def per_device(half_ints, vir_coeffs, occ_energy, vir_energy, roster):
    aux, pair = lax.axis_index("aux"), lax.axis_index("pair")
    rows = jnp.pad(jnp.transpose(vir_coeffs), ((0, 0), (0, 4 * GROUP - vir_coeffs.shape[0])))
    plan = lax.dynamic_slice_in_dim(roster, pair * 2, 2, 0)
    local, paired, _ = front(plan, rows, half_ints)
    flat_local = local.reshape(240, 4096)
    paired = paired.reshape(2, 240, 4096)
    occ_block = lax.dynamic_slice_in_dim(occ_energy, aux * 3, 3, 0)
    vir_block = lax.dynamic_slice_in_dim(vir_energy, pair * 80, 80, 0)
    energy_left = (vir_block[None, :] - occ_block[:, None]).reshape(-1)
    block_plan = lax.dynamic_index_in_dim(roster, aux, 0, keepdims=False)
    density = jnp.zeros((240, 4096), jnp.float32)
    for step in range(2):
        energy_block = lax.dynamic_slice_in_dim(vir_energy, block_plan[step] * 80, 80, 0)
        energy_right = (energy_block[None, :] - occ_block[:, None]).reshape(-1)
        integrals = lax.dot_general(
            flat_local, paired[step], (((1,), (1,)), ((), ())), preferred_element_type=jnp.float32
        )
        amplitudes = (
            spin_scale * integrals / (energy_left[:, None] + energy_right[None, :])
        ).astype(jnp.bfloat16)
        density = density + jnp.dot(amplitudes, paired[step], preferred_element_type=jnp.float32)
    return jnp.transpose(density.astype(jnp.bfloat16).reshape(3, 80, 4096), (1, 0, 2))


def solution(mesh):
    in_specs = (P("pair", None, "aux"), P(None, "aux"), P(), P(), P())
    out_specs = P("pair", "aux", None)
    return jax.shard_map(
        per_device, mesh=mesh, in_specs=in_specs, out_specs=out_specs, check_vma=False
    )
```

time: 498 us -> 198 us (0.40)
  the two profiles are of different devices: /device:TPU:15 before, /device:TPU:87 now
where the time goes in v2:
time: 198 us
  Pallas kernels  175 us (88%)
  matrix products  13.2 us (7%)
  local copies, waits for them, and re-layouts  8.7 us (4%)
    pallas_call x1, Pallas kernels, front(): pl.pallas_call(front_kernel, out_shape=(jax.ShapeDtypeStruct((3, 80, 4096...  175 us
    dot_general x2, matrix products, per_device(): jnp.dot(amplitudes, paired[step], preferred_element_type=jnp.float32)  13.2 us

profile of v2, /device:TPU:87, one launch (start us, length us, event | category | flops | bytes accessed | tf_op | source)
XLA Modules:
  0.0 198.1 jit_solution(9961507529075310820)
XLA Ops:
  0.0 0.0 copy-start
  0.0 0.7 copy-done
  0.7 0.1 constant_dynamic-slice_fusion.1
  0.8 0.6 copy.7.plan
  1.4 1.6 pad.4.rows
  2.9 174.9 %front.1 = (bf16[3,80,4096]{2,1,0:T(8,128)(2,1)}, bf16[6,80,4096]{2,1,0:T(8,128)(2,1)}, bf16[1280,1536]{1,0:T(8,128)(2,1)}) custom-call(s32[2,2]{1,0:T(2,128)} %copy.7.plan, bf16[40,1536]{1,0:T(8,128)(2,1)} %pad.4.rows, bf16[6,1408,128]{2,1,0:T(8,128)(2,1)} %half_hbm.1), custom_call_target="tpu_custom_call" | custom-call | tf_op jit(solution)/shard_map/front/pallas_call | solution.py:321
  177.9 0.0 copy-start.1
  177.9 3.9 %fusion.16 = (bf16[3,80,4096]{2,1,0:T(8,128)(2,1)S(1)}, bf16[3,80,4096]{2,1,0:T(8,128)(2,1)}) fusion(bf16[6,80,4096]{2,1,0:T(8,128)(2,1)} %get-tuple-element.8), kind=kLoop, calls=%fused_computation.24 | loop fusion | bytes 7864320 | tf_op jit(solution)/shard_map/slice | solution.py:364
  181.7 0.1 constant_dynamic-slice_fusion
  181.8 0.6 fusion.18
  183.7 0.9 fusion.17
  184.6 0.0 copy-done.1
  184.6 0.1 dynamic_slice.21
  184.6 0.1 broadcast_subtract_fusion
  184.7 0.1 sub.62
  184.8 0.1 sub.59
  184.9 6.9 %fusion.5 = f32[240,4096]{1,0:T(8,128)} fusion(bf16[240,4096]{1,0:T(8,128)(2,1)} %bitcast.16, bf16[240,4096]{1,0:T(8,128)(2,1)} %bitcast.17, f32[240]{0:T(256)S(1)} %sub.62, f32[240]{0:T(256)S(1)} %sub.59), kind=kOutput, calls=%fused_computation.8 | convolution fusion | flops 943948800 | bytes 7866240 | tf_op jit(solution)/shard_map/dot_general | solution.py:369
  191.8 0.1 sub.65
  191.8 6.3 %fusion = bf16[240,4096]{1,0:T(8,128)(2,1)} fusion(f32[240,4096]{1,0:T(8,128)} %fusion.5, bf16[240,4096]{1,0:T(8,128)(2,1)S(1)} %bitcast.15, bf16[240,4096]{1,0:T(8,128)(2,1)} %bitcast.18, f32[240]{0:T(256)S(1)} %sub.65, f32[240]{0:T(256)S(1)} %sub.59), kind=kOutput, calls=%fused_computation.1 | convolution fusion | flops 945914880 | bytes 9832320 | tf_op jit(solution)/shard_map/dot_general | solution.py:369
Async XLA Ops:
  0.0 0.7 copy-start
  177.9 6.7 %copy-start.1 = (f32[96]{0:T(128)S(1)}, f32[96]{0:T(128)}, u32[]{:S(2)}) copy-start(f32[96]{0:T(128)} %param.7) | copy-start | bytes 1156

commit v3 on v2

--- a/solution.py
+++ b/solution.py
@@ -40,7 +40,6 @@
     w = yl * 2 + core
     side = h * 4 + x
     partner = (aux, pair + 1 - 2 * core)
-    own = pl.ds(pl.multiple_of(aux * 128, 128), 128)
     q_own = pair // 2
 
     half_load = pltpu.make_async_copy(half_hbm, half, half_sem)
@@ -48,17 +47,14 @@
 
     @pl.loop(1, 16)
     def _(d):
-        signal((aux, (pair + d) % 16))
+        signal((((z + d) % 16) * 2 + h, pair))
 
     @pl.loop(1, 32)
     def _(d):
-        signal(((aux + d) % 32, pair))
-
-    @pl.loop(1, 8)
-    def _(d):
-        signal((z * 2 + 1 - h, ((q_own + d) % 8) * 2 + core))
-
-    pl.semaphore_wait(pltpu.get_barrier_semaphore(), 53)
+        other = (h * 16 + pair + d) % 32
+        signal((z * 2 + other // 16, other % 16))
+
+    pl.semaphore_wait(pltpu.get_barrier_semaphore(), 46)
 
     def z_peer(d):
         return (((z + d) % 16) * 2 + h, pair)
@@ -104,52 +100,50 @@
 
         to_partner(yl, side, t).start()
 
-    @pl.loop(0, 4)
-    def _(t):
-        @pl.loop(8, 16)
-        def _(e):
-            to_chip(e, t).start()
-
     half_load.wait()
 
-    def vir_out(v):
-        return remote(vir.at[v], relay.at[pair], send_v.at[v], recv_v.at[pair], (aux, v))
+    def vir_out(v, to_h):
+        return remote(
+            vir.at[v, to_h], relay.at[h, pair], send_v.at[v, to_h], recv_v.at[h, pair], (z * 2 + to_h, v)
+        )
+
+    def stays(v, to_h):
+        return jnp.logical_and(v == pair, to_h == h)
 
     def turn_of(g):
         return (w + (1 - 2 * core) * (g // 2) + 2 * (g % 2)) % 4
 
-    def onward(src, dst, send, recv, plane, to_h, sem):
-        at_home = jnp.logical_and(plane == z, to_h == h)
-
-        @pl.when(at_home)
+    def q_of(array, a):
+        return array.at[:, :, pl.ds(pl.multiple_of(a * 128, 128), 128)]
+
+    def onward(src, dst, send, recv, plane, sem):
+        @pl.when(plane == z)
         def _():
             pltpu.make_async_copy(src, dst, sem).start()
 
-        @pl.when(jnp.logical_not(at_home))
-        def _():
-            remote(src, dst, send, recv, (plane * 2 + to_h, pair)).start()
+        @pl.when(plane != z)
+        def _():
+            remote(src, dst, send, recv, (plane * 2 + h, pair)).start()
+
+    def vir_on(src, plane, from_h):
+        a = z * 2 + from_h
+        onward(src, q_of(local, a), send_x.at[plane, from_h], recv_x.at[a], plane, home_sem.at[from_h])
 
     def forward(g):
-        @pl.loop(0, 4)
+        @pl.loop(0, 8)
         def _(n):
-            plane = ((x + n + z) % 4) * 4 + turn_of(g)
-
-            def both(src):
-                @pl.loop(0, 2)
-                def _(to_h):
-                    onward(
-                        src.at[to_h], local.at[:, :, own], send_x.at[plane * 2 + to_h],
-                        recv_x.at[aux], plane, to_h, home_sem.at[1],
-                    )
-
-            @pl.when(plane == pair)
-            def _():
-                both(vir.at[pair])
-
-            @pl.when(plane != pair)
-            def _():
-                remote(relay.at[plane], relay.at[plane], send_v.at[0], recv_v.at[plane], partner).wait_recv()
-                both(relay.at[plane])
+            plane = ((x + n // 2 + z) % 4) * 4 + turn_of(g)
+            from_h = n % 2
+
+            @pl.when(stays(plane, from_h))
+            def _():
+                vir_on(vir.at[pair, h], plane, from_h)
+
+            @pl.when(jnp.logical_not(stays(plane, from_h)))
+            def _():
+                block = relay.at[from_h, plane]
+                remote(block, block, send_v.at[0, 0], recv_v.at[from_h, plane], partner).wait_recv()
+                vir_on(block, plane, from_h)
 
     @pl.loop(0, 4)
     def _(g):
@@ -186,48 +180,67 @@
             for i in range(6):
                 vir[4 * t + w_now, i // 3, i % 3] = product[80 * t : 80 * t + 80, 128 * i : 128 * i + 128]
 
-        @pl.loop(0, 4)
+        @pl.loop(0, 8)
         def _(n):
-            v = ((x + n + 4 - z % 4) % 4) * 4 + w_now
-
-            @pl.when(v != pair)
-            def _():
-                vir_out(v).start()
+            v = ((x + n // 2 + 4 - z % 4) % 4) * 4 + w_now
+
+            @pl.when(jnp.logical_not(stays(v, n % 2)))
+            def _():
+                vir_out(v, n % 2).start()
 
         @pl.when(g == 0)
         def _():
+            @pl.loop(0, 4)
+            def _(t):
+                @pl.loop(8, 16)
+                def _(e):
+                    to_chip(e, t).start()
+
             forward(0)
 
     for to_h in range(2):
         for step in range(2):
             chosen[to_h, 3 * step : 3 * step + 3] = vir[plan[to_h, step], to_h]
 
-    def chosen_out():
-        return remote(chosen, relay_r, send_w, recv_w, (aux, (pair + z) % 16))
-
-    plane_r = (pair + 16 - z) % 16
-
-    def chosen_on(src):
-        @pl.loop(0, 2)
-        def _(to_h):
-            onward(src.at[to_h], paired.at[:, :, own], send_r.at[to_h], recv_r.at[h], plane_r, to_h, home_sem.at[0])
-
-    @pl.when(z == 0)
-    def _():
-        chosen_on(chosen)
-
-    @pl.when(z != 0)
-    def _():
-        chosen_out().start()
-        chosen_out().wait_recv()
-        chosen_on(relay_r)
+    def column_of(to_h):
+        return (pair + z + 8 * to_h) % 16
+
+    plane_r = (pair + 32 - z - 8 * h) % 16
+
+    def chosen_out(to_h):
+        return remote(
+            chosen.at[to_h], relay_r.at[h], send_w.at[to_h], recv_w.at[h], (z * 2 + to_h, column_of(to_h))
+        )
+
+    @pl.loop(0, 2)
+    def _(to_h):
+        @pl.when(jnp.logical_not(stays(column_of(to_h), to_h)))
+        def _():
+            chosen_out(to_h).start()
+
+    @pl.loop(0, 2)
+    def _(from_h):
+        a = z * 2 + from_h
+
+        def on(src):
+            onward(src, q_of(paired, a), send_r.at[from_h], recv_r.at[from_h], plane_r, home_sem.at[2 + from_h])
+
+        @pl.when(stays(plane_r, from_h))
+        def _():
+            on(chosen.at[h])
+
+        @pl.when(jnp.logical_not(stays(plane_r, from_h)))
+        def _():
+            block = relay_r.at[from_h]
+            remote(block, block, send_w.at[0], recv_w.at[from_h], partner).wait_recv()
+            on(block)
 
     @pl.loop(1, 4)
     def _(g):
         forward(g)
 
     def spread(q, at_core):
-        first = (q * 2 + at_core + 16 - z) % 16
+        first = (q * 2 + at_core + 32 - z - 8 * h) % 16
         return paired.at[:, :, pl.ds(pl.multiple_of(first * 256, 128), 256)]
 
     def spread_out(e):
@@ -236,14 +249,13 @@
 
     @pl.loop(0, 2)
     def _(from_h):
-        home = jnp.logical_and(plane_r == z, from_h == h)
-        part = paired.at[:, :, pl.ds(pl.multiple_of((plane_r * 2 + from_h) * 128, 128), 128)]
-
-        @pl.when(home)
-        def _():
-            pltpu.make_async_copy(chosen.at[0], part, home_sem.at[0]).wait()
-
-        @pl.when(jnp.logical_not(home))
+        part = q_of(paired, plane_r * 2 + from_h)
+
+        @pl.when(plane_r == z)
+        def _():
+            pltpu.make_async_copy(chosen.at[0], part, home_sem.at[2 + from_h]).wait()
+
+        @pl.when(plane_r != z)
         def _():
             remote(part, part, send_r.at[0], recv_r.at[from_h], partner).wait_recv()
 
@@ -286,34 +298,36 @@
         def _(c):
             to_partner(c // 8, c % 8, t).wait_send()
 
-    @pl.when(z != 0)
-    def _():
-        chosen_out().wait_send()
-
-    @pl.loop(0, 16)
-    def _(v):
-        @pl.when(v != pair)
-        def _():
-            vir_out(v).wait_send()
-
     @pl.loop(0, 2)
     def _(to_h):
-        @pl.when(jnp.logical_not(jnp.logical_and(plane_r == z, to_h == h)))
-        def _():
-            part = paired.at[:, :, own]
-            remote(chosen.at[to_h], part, send_r.at[to_h], recv_r.at[0], partner).wait_send()
-
-    @pl.loop(0, 32)
-    def _(a):
-        part = local.at[:, :, pl.ds(pl.multiple_of(a * 128, 128), 128)]
-
-        @pl.when(a == aux)
-        def _():
-            pltpu.make_async_copy(vir.at[0, 0], part, home_sem.at[1]).wait()
-
-        @pl.when(a != aux)
-        def _():
-            remote(vir.at[0, 0], part, send_x.at[a], recv_x.at[a], partner).wait()
+        @pl.when(jnp.logical_not(stays(column_of(to_h), to_h)))
+        def _():
+            chosen_out(to_h).wait_send()
+
+        @pl.when(plane_r != z)
+        def _():
+            part = q_of(paired, 0)
+            remote(chosen.at[0], part, send_r.at[to_h], recv_r.at[0], partner).wait_send()
+
+        @pl.loop(0, 16)
+        def _(v):
+            @pl.when(jnp.logical_not(stays(v, to_h)))
+            def _():
+                vir_out(v, to_h).wait_send()
+
+    @pl.loop(0, 16)
+    def _(plane):
+        @pl.loop(0, 2)
+        def _(from_h):
+            part = q_of(local, plane * 2 + from_h)
+
+            @pl.when(plane == z)
+            def _():
+                pltpu.make_async_copy(vir.at[0, 0], part, home_sem.at[from_h]).wait()
+
+            @pl.when(plane != z)
+            def _():
+                remote(vir.at[0, 0], part, send_x.at[plane, from_h], recv_x.at[plane * 2 + from_h], partner).wait()
 
 
 def front(plan, rows, half):
@@ -331,13 +345,13 @@
             pltpu.VMEM((6, 1408, 128), bf16),
             pltpu.VMEM((4, 80, 1408), bf16),
             pltpu.VMEM((16, 2, 3, 80, 128), bf16),
-            pltpu.VMEM((16, 2, 3, 80, 128), bf16),
+            pltpu.VMEM((2, 16, 3, 80, 128), bf16),
             pltpu.VMEM((2, 6, 80, 128), bf16),
             pltpu.VMEM((2, 6, 80, 128), bf16),
-            DMA, DMA((4,)), DMA((2,)),
+            DMA, DMA((4,)), DMA((4,)),
             DMA((16,)), DMA((4,)), DMA((16, 4)), DMA((16, 4)), DMA((16, 4)), DMA((16, 4)),
-            DMA((16,)), DMA((16,)), DMA, DMA,
-            DMA((32,)), DMA((32,)), DMA((2,)), DMA((2,)),
+            DMA((16, 2)), DMA((2, 16)), DMA((2,)), DMA((2,)),
+            DMA((16, 2)), DMA((32,)), DMA((2,)), DMA((2,)),
             DMA((8,)), DMA((8,)), DMA((8,)), DMA((8,)),
         ],
         compiler_params=pltpu.CompilerParams(collective_id=0, has_side_effects=True),
@@ -345,29 +359,66 @@
     )(plan, rows, half)
 
 
+CHUNKS = 4
+
+
+def density_kernel(left, right, local, paired, out, integrals, amplitudes):
+    g = pl.program_id(0)
+    width = local.shape[2]
+    block = paired[...].reshape(480, width)
+
+    @pl.when(g == 0)
+    def _():
+        integrals[...] = jnp.zeros_like(integrals)
+
+    @pl.when(g < CHUNKS)
+    def _():
+        integrals[...] += lax.dot_general(
+            block, local[...].reshape(240, width), (((1,), (1,)), ((), ())),
+            preferred_element_type=jnp.float32,
+        )
+
+    @pl.when(g == CHUNKS - 1)
+    def _():
+        scaled = spin_scale * jnp.transpose(integrals[...]) / (left[...] + right[...])
+        amplitudes[...] = scaled.astype(jnp.bfloat16)
+
+    @pl.when(g >= CHUNKS)
+    def _():
+        rows = jnp.dot(amplitudes[...], block, preferred_element_type=jnp.float32)
+        out[...] = rows.astype(jnp.bfloat16).reshape(3, 80, width)
+
+
+def density_of(left, right, local, paired):
+    width = 4096 // CHUNKS
+    return pl.pallas_call(
+        density_kernel,
+        out_shape=jax.ShapeDtypeStruct((3, 80, 4096), jnp.bfloat16),
+        grid=(2 * CHUNKS,),
+        in_specs=[
+            pl.BlockSpec((240, 1), lambda g: (0, 0)),
+            pl.BlockSpec((1, 480), lambda g: (0, 0)),
+            pl.BlockSpec((3, 80, width), lambda g: (0, 0, jnp.minimum(g, CHUNKS - 1))),
+            pl.BlockSpec((6, 80, width), lambda g: (0, 0, g % CHUNKS)),
+        ],
+        out_specs=pl.BlockSpec((3, 80, width), lambda g: (0, 0, jnp.maximum(g - CHUNKS, 0))),
+        scratch_shapes=[pltpu.VMEM((480, 240), jnp.float32), pltpu.VMEM((240, 480), jnp.bfloat16)],
+        name="density",
+    )(left, right, local, paired)
+
+
 def per_device(half_ints, vir_coeffs, occ_energy, vir_energy, roster):
     aux, pair = lax.axis_index("aux"), lax.axis_index("pair")
     rows = jnp.pad(jnp.transpose(vir_coeffs), ((0, 0), (0, 4 * GROUP - vir_coeffs.shape[0])))
     plan = lax.dynamic_slice_in_dim(roster, pair * 2, 2, 0)
     local, paired, _ = front(plan, rows, half_ints)
-    flat_local = local.reshape(240, 4096)
-    paired = paired.reshape(2, 240, 4096)
     occ_block = lax.dynamic_slice_in_dim(occ_energy, aux * 3, 3, 0)
     vir_block = lax.dynamic_slice_in_dim(vir_energy, pair * 80, 80, 0)
-    energy_left = (vir_block[None, :] - occ_block[:, None]).reshape(-1)
+    left = (vir_block[None, :] - occ_block[:, None]).reshape(240, 1)
     block_plan = lax.dynamic_index_in_dim(roster, aux, 0, keepdims=False)
-    density = jnp.zeros((240, 4096), jnp.float32)
-    for step in range(2):
-        energy_block = lax.dynamic_slice_in_dim(vir_energy, block_plan[step] * 80, 80, 0)
-        energy_right = (energy_block[None, :] - occ_block[:, None]).reshape(-1)
-        integrals = lax.dot_general(
-            flat_local, paired[step], (((1,), (1,)), ((), ())), preferred_element_type=jnp.float32
-        )
-        amplitudes = (
-            spin_scale * integrals / (energy_left[:, None] + energy_right[None, :])
-        ).astype(jnp.bfloat16)
-        density = density + jnp.dot(amplitudes, paired[step], preferred_element_type=jnp.float32)
-    return jnp.transpose(density.astype(jnp.bfloat16).reshape(3, 80, 4096), (1, 0, 2))
+    rostered = [lax.dynamic_slice_in_dim(vir_energy, block_plan[s] * 80, 80, 0) for s in range(2)]
+    right = jnp.stack([r[None, :] - occ_block[:, None] for r in rostered]).reshape(1, 480)
+    return jnp.transpose(density_of(left, right, local, paired), (1, 0, 2))
 
 
 def solution(mesh):

time: 198 us -> 187 us (0.944)
  the two profiles are of different devices: /device:TPU:87 before, /device:TPU:56 now
where the time goes in v3:
time: 187 us
  Pallas kernels  179 us (96%)
  local copies, waits for them, and re-layouts  5.97 us (3%)
    pallas_call x1, Pallas kernels, front(): pl.pallas_call(front_kernel, out_shape=(jax.ShapeDtypeStruct((3, 80, 4096...  170 us
    pallas_call x1, Pallas kernels, density_of(): pl.pallas_call(density_kernel, out_shape=jax.ShapeDtypeStruct((3, 80, 409...  9.37 us

profile of v3, /device:TPU:56, one launch (start us, length us, event | category | flops | bytes accessed | tf_op | source)
XLA Modules:
  0.0 186.6 jit_solution(2086793472969856576)
XLA Ops:
  0.0 0.0 copy-start
  0.0 0.7 dynamic_slice.20
  0.7 0.0 copy-done
  0.7 0.1 constant_dynamic-slice_fusion
  0.8 0.6 copy.9.plan
  1.4 0.1 constant_dynamic-slice_fusion.1
  1.5 0.5 fusion.1
  3.3 0.9 fusion
  4.2 0.1 broadcast_subtract_fusion.2
  4.3 0.1 broadcast_subtract_fusion.1
  4.4 0.7 reshape.118.right
  5.0 0.8 sub.70.left
  5.8 1.6 pad.4.rows
  7.4 169.8 %front.1 = (bf16[3,80,4096]{2,1,0:T(8,128)(2,1)}, bf16[6,80,4096]{2,1,0:T(8,128)(2,1)}, bf16[1280,1536]{1,0:T(8,128)(2,1)}) custom-call(s32[2,2]{1,0:T(2,128)} %copy.9.plan, bf16[40,1536]{1,0:T(8,128)(2,1)} %pad.4.rows, bf16[6,1408,128]{2,1,0:T(8,128)(2,1)} %half_hbm.1), custom_call_target="tpu_custom_call" | custom-call | tf_op jit(solution)/shard_map/front/pallas_call | solution.py:335
  177.2 9.4 %density.1 = bf16[3,80,4096]{2,1,0:T(8,128)(2,1)} custom-call(f32[240,1]{1,0:T(8,128)} %sub.70.left, f32[1,480]{1,0:T(1,128)} %reshape.118.right, bf16[3,80,4096]{2,1,0:T(8,128)(2,1)} %get-tuple-element.7.local, bf16[6,80,4096]{2,1,0:T(8,128)(2,1)} %get-tuple-element.8.paired), custom_call_target="tpu_custom_call" | custom-call | tf_op jit(solution)/shard_map/density/pallas_call | solution.py:394
  (1 shorter events, 0.0 us)
Async XLA Ops:
  0.0 0.7 copy-start

commit v4 on v3

--- a/solution.py
+++ b/solution.py
@@ -32,8 +32,9 @@
 
 
 def front_kernel(
-    plan, rows, half_hbm, local, paired, columns, half, coeff, vir, relay, chosen, relay_r,
-    half_sem, own_sem, home_sem, send_z, recv_z, send_p, recv_p, send_k, recv_k,
+    roster, rows, half_hbm, local, paired, columns, half, coeff, vir, relay, chosen, relay_r,
+    half_relay, half_own, vir_own, chosen_own, send_s, recv_s, send_t, recv_t, home_t,
+    send_b, recv_b, send_q, recv_q, half_sem, own_sem, home_sem, send_z, recv_z, send_p, recv_p, send_k, recv_k,
     send_v, recv_v, send_w, recv_w, send_x, recv_x, send_r, recv_r, send_g, recv_g, send_c, recv_c,
 ):
     z, h, x, yl, core, aux, pair = place()
@@ -79,6 +80,59 @@
         copy.start()
         copy.wait()
 
+    def stays(v, to_h):
+        return jnp.logical_and(v == pair, to_h == h)
+
+    column = (pair + z + 8 * h) % 16
+
+    def plane_of(from_h):
+        return (pair + 32 - z - 8 * from_h) % 16
+
+    def rows_of(c):
+        return pl.ds(pl.multiple_of(c * 704, 16), 704)
+
+    def half_out(to_h, c):
+        return remote(
+            half_hbm.at[3 * to_h, rows_of(c)], half_relay.at[h, rows_of(c)],
+            send_s.at[to_h, c], recv_s.at[h, c], (z * 2 + to_h, column),
+        )
+
+    def half_on(src, from_h, c):
+        dst = half_own.at[from_h, rows_of(c)]
+        plane = plane_of(from_h)
+
+        @pl.when(plane == z)
+        def _():
+            pltpu.make_async_copy(src, dst, home_t.at[from_h, c]).start()
+
+        @pl.when(plane != z)
+        def _():
+            remote(src, dst, send_t.at[from_h, c], recv_t.at[from_h, c], (plane * 2 + h, pair)).start()
+
+    @pl.loop(0, 2)
+    def _(c):
+        @pl.loop(0, 2)
+        def _(to_h):
+            @pl.when(jnp.logical_not(stays(column, to_h)))
+            def _():
+                half_out(to_h, c).start()
+
+    @pl.loop(0, 2)
+    def _(c):
+        @pl.loop(0, 2)
+        def _(from_h):
+            mine_already = stays(plane_of(from_h), from_h)
+
+            @pl.when(mine_already)
+            def _():
+                half_on(half_hbm.at[3 * h, rows_of(c)], from_h, c)
+
+            @pl.when(jnp.logical_not(mine_already))
+            def _():
+                block = half_relay.at[from_h, rows_of(c)]
+                remote(block, block, send_s.at[0, 0], recv_s.at[from_h, c], partner).wait_recv()
+                half_on(block, from_h, c)
+
     def to_chip(e, t):
         other = (side + e) % 8
         device = (z * 2 + other // 4, (other % 4) * 4 + ((yl + e // 8) % 2) * 2 + core)
@@ -107,9 +161,6 @@
             vir.at[v, to_h], relay.at[h, pair], send_v.at[v, to_h], recv_v.at[h, pair], (z * 2 + to_h, v)
         )
 
-    def stays(v, to_h):
-        return jnp.logical_and(v == pair, to_h == h)
-
     def turn_of(g):
         return (w + (1 - 2 * core) * (g // 2) + 2 * (g % 2)) % 4
 
@@ -127,7 +178,7 @@
 
     def vir_on(src, plane, from_h):
         a = z * 2 + from_h
-        onward(src, q_of(local, a), send_x.at[plane, from_h], recv_x.at[a], plane, home_sem.at[from_h])
+        onward(src, q_of(local.at[pl.ds(1, 2)], a), send_x.at[plane, from_h], recv_x.at[a], plane, home_sem.at[from_h])
 
     def forward(g):
         @pl.loop(0, 8)
@@ -167,18 +218,18 @@
 
         def load(t):
             first = pl.multiple_of((4 * t + w_now) * 80, 16)
-            return pltpu.make_async_copy(columns.at[pl.ds(first, 80), pl.ds(0, 1408)], coeff.at[t], own_sem.at[t])
+            return pltpu.make_async_copy(columns.at[pl.ds(first, 80), pl.ds(0, 1408)], coeff.at[w_now, t], own_sem.at[t])
 
         for t in range(4):
             load(t).start()
         for t in range(4):
             load(t).wait()
-        wide = jnp.concatenate([half[i] for i in range(6)], axis=1)
-        product = jnp.dot(coeff[...].reshape(320, 1408), wide, preferred_element_type=jnp.float32)
+        wide = jnp.concatenate([half[i] for i in (1, 2, 4, 5)], axis=1)
+        product = jnp.dot(coeff[w_now].reshape(320, 1408), wide, preferred_element_type=jnp.float32)
         product = product.astype(jnp.bfloat16)
         for t in range(4):
-            for i in range(6):
-                vir[4 * t + w_now, i // 3, i % 3] = product[80 * t : 80 * t + 80, 128 * i : 128 * i + 128]
+            for i in range(4):
+                vir[4 * t + w_now, i // 2, i % 2] = product[80 * t : 80 * t + 80, 128 * i : 128 * i + 128]
 
         @pl.loop(0, 8)
         def _(n):
@@ -200,21 +251,19 @@
 
     for to_h in range(2):
         for step in range(2):
-            chosen[to_h, 3 * step : 3 * step + 3] = vir[plan[to_h, step], to_h]
-
-    def column_of(to_h):
-        return (pair + z + 8 * to_h) % 16
-
-    plane_r = (pair + 32 - z - 8 * h) % 16
+            block = vir[roster[2 * pair + to_h, step], to_h]
+            chosen[to_h, step] = block[0]
+            chosen[to_h, 2 + step] = block[1]
+
+    def late(array):
+        return array.at[pl.ds(2, 4)]
 
     def chosen_out(to_h):
-        return remote(
-            chosen.at[to_h], relay_r.at[h], send_w.at[to_h], recv_w.at[h], (z * 2 + to_h, column_of(to_h))
-        )
+        return remote(chosen.at[to_h], relay_r.at[h], send_w.at[to_h], recv_w.at[h], (z * 2 + to_h, column))
 
     @pl.loop(0, 2)
     def _(to_h):
-        @pl.when(jnp.logical_not(stays(column_of(to_h), to_h)))
+        @pl.when(jnp.logical_not(stays(column, to_h)))
         def _():
             chosen_out(to_h).start()
 
@@ -223,13 +272,16 @@
         a = z * 2 + from_h
 
         def on(src):
-            onward(src, q_of(paired, a), send_r.at[from_h], recv_r.at[from_h], plane_r, home_sem.at[2 + from_h])
-
-        @pl.when(stays(plane_r, from_h))
+            onward(
+                src, q_of(late(paired), a), send_r.at[from_h], recv_r.at[from_h],
+                plane_of(from_h), home_sem.at[2 + from_h],
+            )
+
+        @pl.when(stays(plane_of(from_h), from_h))
         def _():
             on(chosen.at[h])
 
-        @pl.when(jnp.logical_not(stays(plane_r, from_h)))
+        @pl.when(jnp.logical_not(stays(plane_of(from_h), from_h)))
         def _():
             block = relay_r.at[from_h]
             remote(block, block, send_w.at[0], recv_w.at[from_h], partner).wait_recv()
@@ -239,48 +291,142 @@
     def _(g):
         forward(g)
 
-    def spread(q, at_core):
-        first = (q * 2 + at_core + 32 - z - 8 * h) % 16
-        return paired.at[:, :, pl.ds(pl.multiple_of(first * 256, 128), 256)]
-
-    def spread_out(e):
-        part = spread(q_own, core)
-        return remote(part, part, send_g.at[e], recv_g.at[q_own], (aux, ((q_own + e) % 8) * 2 + core))
+    def column_from(v, from_h):
+        return ((v + 32 - z - 8 * from_h) % 16) * 2 + from_h
+
+    @pl.loop(0, 2)
+    def _(c):
+        @pl.loop(0, 2)
+        def _(from_h):
+            dst = half_own.at[from_h, rows_of(c)]
+
+            @pl.when(plane_of(from_h) == z)
+            def _():
+                pltpu.make_async_copy(half_relay.at[from_h, rows_of(c)], dst, home_t.at[from_h, c]).wait()
+
+            @pl.when(plane_of(from_h) != z)
+            def _():
+                remote(dst, dst, send_t.at[0, 0], recv_t.at[from_h, c], partner).wait_recv()
+
+    @pl.loop(0, 4)
+    def _(g):
+        wide = jnp.concatenate([half_own[0], half_own[1]], axis=1)
+        product = jnp.dot(coeff[g].reshape(320, 1408), wide, preferred_element_type=jnp.float32)
+        product = product.astype(jnp.bfloat16)
+        for t in range(4):
+            for i in range(2):
+                vir_own[4 * t + g, i] = product[80 * t : 80 * t + 80, 128 * i : 128 * i + 128]
+
+    for step in range(2):
+        block = vir_own[roster[aux, step]]
+        chosen_own[0, step] = block[0]
+        chosen_own[1, step] = block[1]
+
+    def early(array):
+        return array.at[pl.ds(0, 2)]
+
+    def own_out(d, from_h):
+        v = (pair + d) % 16
+        a = column_from(pair, from_h)
+        block = remote(
+            vir_own.at[v, from_h], q_of(local, a).at[0], send_b.at[d, from_h], recv_b.at[pair, from_h], (aux, v)
+        )
+        picked = remote(
+            chosen_own.at[from_h], q_of(early(paired), a), send_q.at[d, from_h], recv_q.at[pair, from_h], (aux, v)
+        )
+        return block, picked
+
+    def own_kept(from_h):
+        a = column_from(pair, from_h)
+        return (
+            pltpu.make_async_copy(vir_own.at[pair, from_h], q_of(local, a).at[0], send_b.at[0, from_h]),
+            pltpu.make_async_copy(chosen_own.at[from_h], q_of(early(paired), a), send_q.at[0, from_h]),
+        )
 
     @pl.loop(0, 2)
     def _(from_h):
-        part = q_of(paired, plane_r * 2 + from_h)
-
-        @pl.when(plane_r == z)
+        for copy in own_kept(from_h):
+            copy.start()
+
+        @pl.loop(1, 16)
+        def _(d):
+            for copy in own_out(d, from_h):
+                copy.start()
+
+    def spread(q, at_core, from_h):
+        return q_of(late(paired), column_from(q * 2 + at_core, from_h))
+
+    def spread_out(e, from_h):
+        part = spread(q_own, core, from_h)
+        device = (aux, ((q_own + e) % 8) * 2 + core)
+        return remote(part, part, send_g.at[e, from_h], recv_g.at[q_own, from_h], device)
+
+    def spread_over(q, at_core, from_h):
+        part = spread(q, at_core, from_h)
+        return remote(part, part, send_c.at[q, from_h], recv_c.at[q, from_h], partner)
+
+    @pl.loop(0, 2)
+    def _(from_h):
+        part = spread(q_own, core, from_h)
+
+        @pl.when(plane_of(from_h) == z)
         def _():
             pltpu.make_async_copy(chosen.at[0], part, home_sem.at[2 + from_h]).wait()
 
-        @pl.when(plane_r != z)
+        @pl.when(plane_of(from_h) != z)
         def _():
             remote(part, part, send_r.at[0], recv_r.at[from_h], partner).wait_recv()
 
-    @pl.loop(1, 8)
-    def _(e):
-        spread_out(e).start()
-
-    part = spread(q_own, core)
-    remote(part, part, send_c.at[q_own], recv_c.at[q_own], partner).start()
-
-    @pl.loop(1, 8)
-    def _(e):
-        q = (q_own + 8 - e) % 8
-        part = spread(q, core)
-        remote(part, part, send_c.at[q], recv_g.at[q], partner).wait_recv()
-        remote(part, part, send_c.at[q], recv_c.at[q], partner).start()
-
-    @pl.loop(0, 8)
-    def _(q):
-        part = spread(q, 1 - core)
-        remote(part, part, send_c.at[q], recv_c.at[q], partner).wait()
-
-    @pl.loop(1, 8)
-    def _(e):
-        spread_out(e).wait_send()
+        @pl.loop(1, 8)
+        def _(e):
+            spread_out(e, from_h).start()
+
+        spread_over(q_own, core, from_h).start()
+
+    @pl.loop(0, 2)
+    def _(from_h):
+        @pl.loop(1, 8)
+        def _(e):
+            q = (q_own + 8 - e) % 8
+            part = spread(q, core, from_h)
+            remote(part, part, send_c.at[q, 0], recv_g.at[q, from_h], partner).wait_recv()
+            spread_over(q, core, from_h).start()
+
+    @pl.loop(0, 2)
+    def _(from_h):
+        @pl.loop(0, 8)
+        def _(q):
+            spread_over(q, 1 - core, from_h).wait()
+
+    @pl.loop(0, 2)
+    def _(from_h):
+        @pl.loop(1, 8)
+        def _(e):
+            spread_out(e, from_h).wait_send()
+
+        for copy in own_kept(from_h):
+            copy.wait()
+
+        @pl.loop(1, 16)
+        def _(d):
+            for copy in own_out(d, from_h):
+                copy.wait_send()
+            v = (pair + d) % 16
+            a = column_from(v, from_h)
+            block, picked = q_of(local, a).at[0], q_of(early(paired), a)
+            remote(block, block, send_b.at[0, 0], recv_b.at[v, from_h], partner).wait_recv()
+            remote(picked, picked, send_b.at[0, 0], recv_q.at[v, from_h], partner).wait_recv()
+
+        @pl.loop(0, 2)
+        def _(c):
+            @pl.when(jnp.logical_not(stays(column, from_h)))
+            def _():
+                half_out(from_h, c).wait_send()
+
+            @pl.when(plane_of(from_h) != z)
+            def _():
+                part = half_own.at[from_h, rows_of(c)]
+                remote(part, part, send_t.at[from_h, c], recv_t.at[0, 0], partner).wait_send()
 
     @pl.when(owner)
     def _():
@@ -300,13 +446,13 @@
 
     @pl.loop(0, 2)
     def _(to_h):
-        @pl.when(jnp.logical_not(stays(column_of(to_h), to_h)))
+        @pl.when(jnp.logical_not(stays(column, to_h)))
         def _():
             chosen_out(to_h).wait_send()
 
-        @pl.when(plane_r != z)
-        def _():
-            part = q_of(paired, 0)
+        @pl.when(plane_of(to_h) != z)
+        def _():
+            part = q_of(late(paired), 0)
             remote(chosen.at[0], part, send_r.at[to_h], recv_r.at[0], partner).wait_send()
 
         @pl.loop(0, 16)
@@ -319,7 +465,7 @@
     def _(plane):
         @pl.loop(0, 2)
         def _(from_h):
-            part = q_of(local, plane * 2 + from_h)
+            part = q_of(local.at[pl.ds(1, 2)], plane * 2 + from_h)
 
             @pl.when(plane == z)
             def _():
@@ -330,7 +476,7 @@
                 remote(vir.at[0, 0], part, send_x.at[plane, from_h], recv_x.at[plane * 2 + from_h], partner).wait()
 
 
-def front(plan, rows, half):
+def front(roster, rows, half):
     bf16 = jnp.bfloat16
     return pl.pallas_call(
         front_kernel,
@@ -343,20 +489,26 @@
         out_specs=(ANY, ANY, ANY),
         scratch_shapes=[
             pltpu.VMEM((6, 1408, 128), bf16),
-            pltpu.VMEM((4, 80, 1408), bf16),
-            pltpu.VMEM((16, 2, 3, 80, 128), bf16),
-            pltpu.VMEM((2, 16, 3, 80, 128), bf16),
-            pltpu.VMEM((2, 6, 80, 128), bf16),
-            pltpu.VMEM((2, 6, 80, 128), bf16),
+            pltpu.VMEM((4, 4, 80, 1408), bf16),
+            pltpu.VMEM((16, 2, 2, 80, 128), bf16),
+            pltpu.VMEM((2, 16, 2, 80, 128), bf16),
+            pltpu.VMEM((2, 4, 80, 128), bf16),
+            pltpu.VMEM((2, 4, 80, 128), bf16),
+            pltpu.VMEM((2, 1408, 128), bf16),
+            pltpu.VMEM((2, 1408, 128), bf16),
+            pltpu.VMEM((16, 2, 80, 128), bf16),
+            pltpu.VMEM((2, 2, 80, 128), bf16),
+            DMA((2, 2)), DMA((2, 2)), DMA((2, 2)), DMA((2, 2)), DMA((2, 2)),
+            DMA((16, 2)), DMA((16, 2)), DMA((16, 2)), DMA((16, 2)),
             DMA, DMA((4,)), DMA((4,)),
             DMA((16,)), DMA((4,)), DMA((16, 4)), DMA((16, 4)), DMA((16, 4)), DMA((16, 4)),
             DMA((16, 2)), DMA((2, 16)), DMA((2,)), DMA((2,)),
             DMA((16, 2)), DMA((32,)), DMA((2,)), DMA((2,)),
-            DMA((8,)), DMA((8,)), DMA((8,)), DMA((8,)),
+            DMA((8, 2)), DMA((8, 2)), DMA((8, 2)), DMA((8, 2)),
         ],
         compiler_params=pltpu.CompilerParams(collective_id=0, has_side_effects=True),
         name="front",
-    )(plan, rows, half)
+    )(roster, rows, half)
 
 
 CHUNKS = 4
@@ -410,14 +562,13 @@
 def per_device(half_ints, vir_coeffs, occ_energy, vir_energy, roster):
     aux, pair = lax.axis_index("aux"), lax.axis_index("pair")
     rows = jnp.pad(jnp.transpose(vir_coeffs), ((0, 0), (0, 4 * GROUP - vir_coeffs.shape[0])))
-    plan = lax.dynamic_slice_in_dim(roster, pair * 2, 2, 0)
-    local, paired, _ = front(plan, rows, half_ints)
+    local, paired, _ = front(roster, rows, half_ints)
     occ_block = lax.dynamic_slice_in_dim(occ_energy, aux * 3, 3, 0)
     vir_block = lax.dynamic_slice_in_dim(vir_energy, pair * 80, 80, 0)
     left = (vir_block[None, :] - occ_block[:, None]).reshape(240, 1)
     block_plan = lax.dynamic_index_in_dim(roster, aux, 0, keepdims=False)
     rostered = [lax.dynamic_slice_in_dim(vir_energy, block_plan[s] * 80, 80, 0) for s in range(2)]
-    right = jnp.stack([r[None, :] - occ_block[:, None] for r in rostered]).reshape(1, 480)
+    right = (jnp.stack(rostered)[None] - occ_block[:, None, None]).reshape(1, 480)
     return jnp.transpose(density_of(left, right, local, paired), (1, 0, 2))
 
 

time: 187 us -> 169 us (0.904)
  Pallas kernels: 179 us -> 159 us
    pallas_call x1, Pallas kernels: 170 us -> 149 us  [front(): pl.pallas_call(front_kernel, out_shape=(jax.ShapeDtypeStruct((3, 80, 4096...]
where the time goes in v4:
time: 169 us; the launch traced here: 167 us
  Pallas kernels  159 us (94%)
  local copies, waits for them, and re-layouts  7.34 us (4%)
    pallas_call x1, Pallas kernels, front(): pl.pallas_call(front_kernel, out_shape=(jax.ShapeDtypeStruct((3, 80, 4096...  149 us
    pallas_call x1, Pallas kernels, density_of(): pl.pallas_call(density_kernel, out_shape=jax.ShapeDtypeStruct((3, 80, 409...  9.37 us

profile of v4, /device:TPU:56, one launch (start us, length us, event | category | flops | bytes accessed | tf_op | source)
XLA Modules:
  0.0 167.5 jit_solution(7869527508238420890)
XLA Ops:
  0.0 0.7 dynamic_slice.17
  0.7 0.7 constant_dynamic-slice_fusion
  1.5 0.6 fusion
  3.4 0.9 dynamic-slice_bitcast_fusion.1
  4.3 0.1 broadcast_subtract_fusion
  4.3 0.7 sub.53.right
  5.0 0.1 broadcast_subtract_fusion.1
  5.1 1.4 copy.7.roster
  6.4 0.8 sub.54.left
  7.2 1.6 pad.4.rows
  8.8 149.3 %front.1 = (bf16[3,80,4096]{2,1,0:T(8,128)(2,1)}, bf16[6,80,4096]{2,1,0:T(8,128)(2,1)}, bf16[1280,1536]{1,0:T(8,128)(2,1)}) custom-call(s32[32,2]{1,0:T(8,128)} %copy.7.roster, bf16[40,1536]{1,0:T(8,128)(2,1)} %pad.4.rows, bf16[6,1408,128]{2,1,0:T(8,128)(2,1)} %half_hbm.1), custom_call_target="tpu_custom_call" | custom-call | tf_op jit(solution)/shard_map/front/pallas_call | solution.py:481
  158.1 9.4 %density.1 = bf16[3,80,4096]{2,1,0:T(8,128)(2,1)} custom-call(f32[240,1]{1,0:T(8,128)} %sub.54.left, f32[1,480]{1,0:T(1,128)} %sub.53.right, bf16[3,80,4096]{2,1,0:T(8,128)(2,1)} %get-tuple-element.7.local, bf16[6,80,4096]{2,1,0:T(8,128)(2,1)} %get-tuple-element.8.paired), custom_call_target="tpu_custom_call" | custom-call | tf_op jit(solution)/shard_map/density/pallas_call | solution.py:546
  (1 shorter events, 0.0 us)

commit v5 on v4

--- a/solution.py
+++ b/solution.py
@@ -32,7 +32,7 @@
 
 
 def front_kernel(
-    roster, rows, half_hbm, local, paired, columns, half, coeff, vir, relay, chosen, relay_r,
+    roster, rows_hbm, half_hbm, local, paired, columns, rows, half, coeff, vir, relay, chosen, relay_r,
     half_relay, half_own, vir_own, chosen_own, send_s, recv_s, send_t, recv_t, home_t,
     send_b, recv_b, send_q, recv_q, half_sem, own_sem, home_sem, send_z, recv_z, send_p, recv_p, send_k, recv_k,
     send_v, recv_v, send_w, recv_w, send_x, recv_x, send_r, recv_r, send_g, recv_g, send_c, recv_c,
@@ -45,6 +45,9 @@
 
     half_load = pltpu.make_async_copy(half_hbm, half, half_sem)
     half_load.start()
+    rows_load = pltpu.make_async_copy(rows_hbm, rows.at[:, pl.ds(0, 1408)], home_sem.at[0])
+    rows_load.start()
+    rows[:, 1408:] = jnp.zeros((40, 4 * GROUP - 1408), jnp.bfloat16)
 
     @pl.loop(1, 16)
     def _(d):
@@ -55,6 +58,7 @@
         other = (h * 16 + pair + d) % 32
         signal((z * 2 + other // 16, other % 16))
 
+    rows_load.wait()
     pl.semaphore_wait(pltpu.get_barrier_semaphore(), 46)
 
     def z_peer(d):
@@ -251,7 +255,7 @@
 
     for to_h in range(2):
         for step in range(2):
-            block = vir[roster[2 * pair + to_h, step], to_h]
+            block = vir[roster[step, 2 * pair + to_h], to_h]
             chosen[to_h, step] = block[0]
             chosen[to_h, 2 + step] = block[1]
 
@@ -318,7 +322,7 @@
                 vir_own[4 * t + g, i] = product[80 * t : 80 * t + 80, 128 * i : 128 * i + 128]
 
     for step in range(2):
-        block = vir_own[roster[aux, step]]
+        block = vir_own[roster[step, aux]]
         chosen_own[0, step] = block[0]
         chosen_own[1, step] = block[1]
 
@@ -488,6 +492,7 @@
         in_specs=[pl.BlockSpec(memory_space=pltpu.SMEM), ANY, ANY],
         out_specs=(ANY, ANY, ANY),
         scratch_shapes=[
+            pltpu.VMEM((40, 4 * GROUP), bf16),
             pltpu.VMEM((6, 1408, 128), bf16),
             pltpu.VMEM((4, 4, 80, 1408), bf16),
             pltpu.VMEM((16, 2, 2, 80, 128), bf16),
@@ -511,7 +516,7 @@
     )(roster, rows, half)
 
 
-CHUNKS = 4
+CHUNKS = 2
 
 
 def density_kernel(left, right, local, paired, out, integrals, amplitudes):
@@ -561,8 +566,8 @@
 
 def per_device(half_ints, vir_coeffs, occ_energy, vir_energy, roster):
     aux, pair = lax.axis_index("aux"), lax.axis_index("pair")
-    rows = jnp.pad(jnp.transpose(vir_coeffs), ((0, 0), (0, 4 * GROUP - vir_coeffs.shape[0])))
-    local, paired, _ = front(roster, rows, half_ints)
+    rows = jnp.transpose(vir_coeffs)
+    local, paired, _ = front(jnp.transpose(roster), rows, half_ints)
     occ_block = lax.dynamic_slice_in_dim(occ_energy, aux * 3, 3, 0)
     vir_block = lax.dynamic_slice_in_dim(vir_energy, pair * 80, 80, 0)
     left = (vir_block[None, :] - occ_block[:, None]).reshape(240, 1)

time: 169 us -> 164 us (0.970)
  local copies, waits for them, and re-layouts: 7.34 us -> 4.41 us
  Pallas kernels: 159 us -> 157 us
    pallas_call x1, Pallas kernels: 9.37 us -> 7.38 us  [density_of(): pl.pallas_call(density_kernel, out_shape=jax.ShapeDtypeStruct((3, 80, 409...]
where the time goes in v5:
time: 164 us; the launch traced here: 163 us
  Pallas kernels  157 us (96%)
  local copies, waits for them, and re-layouts  4.41 us (3%)
    pallas_call x1, Pallas kernels, front(): pl.pallas_call(front_kernel, out_shape=(jax.ShapeDtypeStruct((3, 80, 4096...  150 us
    pallas_call x1, Pallas kernels, density_of(): pl.pallas_call(density_kernel, out_shape=jax.ShapeDtypeStruct((3, 80, 409...  7.38 us

profile of v5, /device:TPU:56, one launch (start us, length us, event | category | flops | bytes accessed | tf_op | source)
XLA Modules:
  0.0 163.2 jit_solution(12016178567852806539)
XLA Ops:
  0.0 0.7 dynamic_slice.17
  0.7 0.7 constant_dynamic-slice_fusion
  1.5 0.6 fusion
  3.4 0.9 dynamic-slice_bitcast_fusion.1
  4.3 0.1 broadcast_subtract_fusion
  4.3 0.7 sub.53.right
  5.0 0.1 broadcast_subtract_fusion.1
  5.1 0.8 sub.54.left
  5.9 149.9 %front.1 = (bf16[3,80,4096]{2,1,0:T(8,128)(2,1)}, bf16[6,80,4096]{2,1,0:T(8,128)(2,1)}, bf16[1280,1536]{1,0:T(8,128)(2,1)}) custom-call(s32[2,32]{1,0:T(2,128)} %bitcast.10, bf16[40,1408]{1,0:T(8,128)(2,1)} %bitcast.9, bf16[6,1408,128]{2,1,0:T(8,128)(2,1)} %half_hbm.1), custom_call_target="tpu_custom_call" | custom-call | tf_op jit(solution)/shard_map/front/pallas_call | solution.py:485
  155.8 7.4 %density.1 = bf16[3,80,4096]{2,1,0:T(8,128)(2,1)} custom-call(f32[240,1]{1,0:T(8,128)} %sub.54.left, f32[1,480]{1,0:T(1,128)} %sub.53.right, bf16[3,80,4096]{2,1,0:T(8,128)(2,1)} %get-tuple-element.7.local, bf16[6,80,4096]{2,1,0:T(8,128)(2,1)} %get-tuple-element.8.paired), custom_call_target="tpu_custom_call" | custom-call | tf_op jit(solution)/shard_map/density/pallas_call | solution.py:551
  (1 shorter events, 0.0 us)
